TPU v7x, 512 devices: a whole 4x4x16 slice. The times are simulated.
512 devices in a mesh: event: 8 (over y, core), tile: 64 (over x, z).
Axes of the slice: x: 4, y: 4, z: 16, core: 2. Of those that a mesh axis runs over, the one named last changes fastest.
Arguments:
- surface_start: float32 [8, 512, 8192], P('event', 'tile'), may hold values from -6 to 6
- east_start: float32 [8, 512, 8192], P('event', 'tile'), may hold values from -5 to 5
- north_start: float32 [8, 512, 8192], P('event', 'tile'), may hold values from -5 to 5
- still_depth: float32 [512, 8192], P('tile'), may hold values from 1 to 4
- roughness: float32 [512, 8192], P('tile'), may hold values from 0.5 to 2
- wet_masks: int32 [8, 2, 512, 8192], P('event', None, 'tile'), may hold values 0 or 1
- gauge_tiles: int32 [8, 16384, 1], P('event', 'tile'), may hold values from 0 to 63; in each aligned block of 256 rows (0 to 255, 256 to 511, ..., all dimensions but the last counted through in order) at most 8 rows name the same one
- gauge_cells: int32 [8, 16384], P('event', 'tile'), may hold values from 0 to 65535
- gauge_values: float32 [8, 16384], P('event', 'tile'), may hold values from -6 to 6
- survey_surface: float32 [8, 512, 8192], P('event', 'tile'), may hold values from -6 to 6
Outputs:
- roughness_grad: float32 [512, 8192], P('tile', 'event')
Inputs may be any that keep to these rules, and one draw needn't show every extreme that they name: `gauge_tiles`: of the gauges of one event listed on one strip, at most 8 lie in any one strip, and some strip receives exactly 8.
All inputs are finite; a program needn't handle non-finite values. No bound on the sum of `wet_masks` on one device may be relied on, other than what follows from the above.
Results may differ from a plain program's by a relative error of at most 0.0003.
Values sent between devices are 32-bit elements; how exact they have to be, the bound alone decides.
No kernel may reach another device: no remote copies, remote signals or barrier semaphores. Data moves between devices by JAX's collectives and lax.ppermute only.
A program may use at most 64 MiB of HBM per device.

v0:
```python
import jax
import jax.numpy as jnp
from jax import lax
from jax.sharding import PartitionSpec as P

STEPS = 2


def shifted(value, axis, steps):
    count = lax.axis_size(axis)
    initial, last = (max(0, -steps), min(count, count - steps))
    return lax.ppermute(value, axis, [(source, source + steps) for source in range(initial, last)])


def padded_2(cells, sides, width):
    for axis, dim in sides:
        count = lax.axis_size(axis)
        ends = count - 1
        head = lax.slice_in_dim(cells, 0, width, axis=dim)
        tail = lax.slice_in_dim(cells, cells.shape[dim] - width, cells.shape[dim], axis=dim)
        cells = jnp.concatenate(
            [
                lax.ppermute(tail, axis, [(i, (i + 1) % count) for i in range(ends)]),
                cells,
                lax.ppermute(head, axis, [((i + 1) % count, i) for i in range(ends)]),
            ],
            axis=dim,
        )
    return cells


def interior(field):
    return field[1:-1]


def across(field):
    padded = jnp.pad(field, ((0, 0), (1, 1)))
    return padded[:, 2:] - padded[:, :-2]


def along(field):
    return field[2:] - field[:-2]


def advance(surface, east, north, depth_rows, rough_rows, wetness):
    depth_inner = interior(depth_rows)
    depth_safe = jnp.where(depth_inner > 0, depth_inner, 1.0)
    east_inner = interior(east)
    north_inner = interior(north)
    speed = jnp.sqrt(east_inner * east_inner + north_inner * north_inner + 1.0)
    rough_inner = interior(rough_rows)
    friction = 1.0 + 2.0 * rough_inner * rough_inner * speed / depth_safe ** (4.0 / 3.0)
    wet_inner = interior(wetness)
    new_east = wet_inner * (east_inner - 0.2 * depth_inner * across(interior(surface))) / friction
    new_north = wet_inner * (north_inner - 0.2 * depth_inner * along(surface)) / friction
    new_surface = interior(interior(surface)) - 0.25 * interior(wet_inner) * (
        interior(across(new_east)) + along(new_north)
    )
    return (new_surface, interior(new_east), interior(new_north))


def fold_rims(stacked, width):
    upper = stacked[:, :width]
    lower = stacked[:, stacked.shape[1] - width :]
    inner = stacked[:, width : stacked.shape[1] - width]
    from_below = shifted(upper, "tile", -1)
    from_above = shifted(lower, "tile", 1)
    inner = inner.at[:, inner.shape[1] - width :].add(from_below)
    return inner.at[:, :width].add(from_above)


def per_device(
    surface_start,
    east_start,
    north_start,
    still_depth,
    roughness,
    wet_masks,
    gauge_tiles,
    gauge_cells,
    gauge_values,
    survey_surface,
):
    row_count, col_count = still_depth.shape
    wet_float = wet_masks[0].astype(jnp.float32)
    statics = jnp.stack((still_depth, roughness))
    stored = []
    width = 2
    static_pad = padded_2(statics, (("tile", 1),), 2)
    surface, east, north = (surface_start[0], east_start[0], north_start[0])
    for step_index in range(STEPS):
        padded = padded_2(
            jnp.stack((surface, east, north, wet_float[step_index])), (("tile", 1),), 2
        )
        record = (padded[0], padded[1], padded[2], static_pad[0], static_pad[1], padded[3])
        stored.append(record)
        surface, east, north = advance(*record)
    strip_tiles = gauge_tiles[0, :, 0]
    tile_count = lax.axis_size("tile")
    listed = strip_tiles.shape[0]
    capacity = max(2, 2 * listed // tile_count)
    onehot = (strip_tiles[:, None] == jnp.arange(tile_count, dtype=jnp.int32)[None, :]).astype(
        jnp.int32
    )
    before = jnp.cumsum(onehot, axis=0) - onehot
    rank = jnp.sum(onehot * before, axis=1)
    slot = strip_tiles * capacity + rank
    cell_count = row_count * col_count
    send_cells = (
        jnp.full((tile_count * capacity,), cell_count, jnp.int32).at[slot].set(gauge_cells[0])
    )
    send_values = jnp.zeros((tile_count * capacity,), jnp.float32).at[slot].set(gauge_values[0])
    got_cells, got_values = (
        lax.all_to_all(
            send_cells.reshape(tile_count, capacity),
            "tile",
            split_axis=0,
            concat_axis=0,
            tiled=True,
        ),
        lax.all_to_all(
            send_values.reshape(tile_count, capacity),
            "tile",
            split_axis=0,
            concat_axis=0,
            tiled=True,
        ),
    )
    flat_cells = got_cells.reshape(-1)
    valid = flat_cells < cell_count
    seen = jnp.take(surface.reshape(-1), flat_cells, mode="fill", fill_value=0.0)
    missing = jnp.where(valid, seen - got_values.reshape(-1), 0.0)
    gauge_sense = (
        jnp.zeros((cell_count,), jnp.float32)
        .at[flat_cells]
        .add(missing, mode="drop")
        .reshape(row_count, col_count)
    )
    sense_surface = gauge_sense + (surface - survey_surface[0])
    sense_east = jnp.zeros_like(sense_surface)
    sense_north = jnp.zeros_like(sense_surface)
    rough_sense = jnp.zeros((row_count + 2 * width, col_count), jnp.float32)
    for step_index in reversed(range(STEPS)):
        surface_in, east_in, north_in, depth_rows, rough_rows, wetness = stored[step_index]

        def local_step(surface_arg, east_arg, north_arg, rough_arg):
            return advance(surface_arg, east_arg, north_arg, depth_rows, rough_arg, wetness)

        outputs, pullback = jax.vjp(local_step, surface_in, east_in, north_in, rough_rows)
        back_surface, back_east, back_north, back_rough = pullback(
            (sense_surface, sense_east, sense_north)
        )
        rough_sense = rough_sense + back_rough
        if step_index > 0:
            folded = fold_rims(jnp.stack((back_surface, back_east, back_north)), 2)
            sense_surface, sense_east, sense_north = (folded[0], folded[1], folded[2])
    local_grad = fold_rims(rough_sense[None], width)[0]
    total = lax.psum(local_grad, "event")
    share = col_count // lax.axis_size("event")
    return lax.dynamic_slice_in_dim(total, lax.axis_index("event") * share, share, 1)


def solution(mesh):
    placed = (
        P("event", "tile", None),
        P("event", "tile", None),
        P("event", "tile", None),
        P("tile", None),
        P("tile", None),
        P("event", None, "tile", None),
        P("event", "tile", None),
        P("event", "tile"),
        P("event", "tile"),
        P("event", "tile", None),
    )
    return jax.shard_map(
        per_device, mesh=mesh, in_specs=placed, out_specs=P("tile", "event"), check_vma=False
    )
```

profile of v0, /device:TPU:2, one launch (start us, length us, event | category | flops | bytes accessed | tf_op | source)
XLA Modules:
  0.0 217.5 jit_solution(9492636156233918174)
XLA Ops:
  6.5 1.4 pad_maximum_fusion.31
  7.9 3.8 %collective-permute-start = (f32[2,2,8192]{2,1,0:T(2,128)S(1)}, f32[2,2,8192]{2,1,0:T(2,128)S(1)}, u32[]{:S(2)}, u32[]{:S(2)}) collective-permute-start(f32[2,2,8192]{2,1,0:T(2,128)S(1)} %get-tuple-element.102), channel_id=1, source_target_pairs={{0,1},{1,2},{2,3},{3,4},{4,5},{5,6},{6,7},{7,8},{8,9},{9,10},{10,1... | collective-permute-start | bytes 393224 | tf_op jit(solution)/shard_map/ppermute | solution.py:23
  11.7 9.5 %collective-permute-start.1 = (f32[2,2,8192]{2,1,0:T(2,128)S(1)}, f32[2,2,8192]{2,1,0:T(2,128)}, u32[]{:S(2)}, u32[]{:S(2)}) collective-permute-start(f32[2,2,8192]{2,1,0:T(2,128)S(1)} %get-tuple-element.103), channel_id=1, source_target_pairs={{1,0},{2,1},{3,2},{4,3},{5,4},{6,5},{7,6},{8,7},{9,8},{10,9},{11,1... | collective-permute-start | bytes 393224 | tf_op jit(solution)/shard_map/ppermute | solution.py:25
  21.2 0.7 fusion.44
  22.7 0.8 fusion.40
  24.2 1.6 scatter_custom_fusion
  25.8 0.7 all_to_all.12
  26.5 12.4 %all-to-all-start = ((s32[64,1,8]{2,1,0:T(1,128)}), s32[64,1,8]{2,1,0:T(1,128)S(1)}, u32[]{:S(2)}, u32[]{:S(2)}) async-start(s32[64,1,8]{2,1,0:T(1,128)} %bitcast.12), calls=%async_computation | async-start | bytes 65536 | tf_op jit(solution)/shard_map/all_to_all | solution.py:114
  38.9 1.1 convert_element_type.19
  40.0 1.6 scatter_custom_fusion.1
  41.6 0.7 all_to_all.14
  42.3 10.1 %all-to-all-done = s32[64,1,8]{2,1,0:T(1,128)S(1)} async-done(((s32[64,1,8]{2,1,0:T(1,128)}), s32[64,1,8]{2,1,0:T(1,128)S(1)}, u32[]{:S(2)}, u32[]{:S(2)}) %all-to-all-start) | async-done | bytes 2080 | tf_op jit(solution)/shard_map/all_to_all | solution.py:114
  52.4 5.5 %all-to-all-start.1 = ((f32[64,1,8]{2,1,0:T(1,128)}), f32[64,1,8]{2,1,0:T(1,128)S(1)}, u32[]{:S(2)}, u32[]{:S(2)}) async-start(f32[64,1,8]{2,1,0:T(1,128)} %bitcast.32), calls=%async_computation.1 | async-start | bytes 65536 | tf_op jit(solution)/shard_map/all_to_all | solution.py:121
  57.9 1.0 pad_maximum_fusion.27
  58.9 3.4 %collective-permute-start.2 = (f32[4,2,8192]{2,1,0:T(2,128)}, f32[4,2,8192]{2,1,0:T(2,128)S(1)}, u32[]{:S(2)}, u32[]{:S(2)}) collective-permute-start(f32[4,2,8192]{2,1,0:T(2,128)} %get-tuple-element.88), channel_id=1, source_target_pairs={{0,1},{1,2},{2,3},{3,4},{4,5},{5,6},{6,7},{7,8},{8,9},{9,10},{10,1... | collective-permute-start | bytes 786440 | tf_op jit(solution)/shard_map/ppermute | solution.py:23
  62.2 4.6 %collective-permute-start.3 = (f32[4,2,8192]{2,1,0:T(2,128)}, f32[4,2,8192]{2,1,0:T(2,128)S(1)}, u32[]{:S(2)}, u32[]{:S(2)}) collective-permute-start(f32[4,2,8192]{2,1,0:T(2,128)} %get-tuple-element.89), channel_id=1, source_target_pairs={{1,0},{2,1},{3,2},{4,3},{5,4},{6,5},{7,6},{8,7},{9,8},{10,9},{11,1... | collective-permute-start | bytes 786440 | tf_op jit(solution)/shard_map/ppermute | solution.py:25
  67.4 0.7 reduce.18
  68.3 3.0 %all-to-all-done.1 = f32[64,1,8]{2,1,0:T(1,128)S(1)} async-done(((f32[64,1,8]{2,1,0:T(1,128)}), f32[64,1,8]{2,1,0:T(1,128)S(1)}, u32[]{:S(2)}, u32[]{:S(2)}) %all-to-all-start.1) | async-done | bytes 2080 | tf_op jit(solution)/shard_map/all_to_all | solution.py:121
  71.9 0.7 reduce.19
  72.7 1.3 pad_maximum_fusion.3
  74.7 0.7 copy-done.20
  75.8 2.0 fusion.58
  77.9 1.4 pad_slice_fusion.3
  79.6 2.6 %collective-permute-start.4 = (f32[4,2,8192]{2,1,0:T(2,128)S(1)}, f32[4,2,8192]{2,1,0:T(2,128)S(1)}, u32[]{:S(2)}, u32[]{:S(2)}) collective-permute-start(f32[4,2,8192]{2,1,0:T(2,128)S(1)} %get-tuple-element.86), channel_id=1, source_target_pairs={{0,1},{1,2},{2,3},{3,4},{4,5},{5,6},{6,7},{7,8},{8,9},{9,10},{10,1... | collective-permute-start | bytes 786440 | tf_op jit(solution)/shard_map/ppermute | solution.py:23
  82.2 5.5 %collective-permute-start.5 = (f32[4,2,8192]{2,1,0:T(2,128)S(1)}, f32[4,2,8192]{2,1,0:T(2,128)S(1)}, u32[]{:S(2)}, u32[]{:S(2)}) collective-permute-start(f32[4,2,8192]{2,1,0:T(2,128)S(1)} %get-tuple-element.87), channel_id=1, source_target_pairs={{1,0},{2,1},{3,2},{4,3},{5,4},{6,5},{7,6},{8,7},{9,8},{10,9},{11,1... | collective-permute-start | bytes 786440 | tf_op jit(solution)/shard_map/ppermute | solution.py:25
  87.8 2.2 %collective-permute-done.4 = f32[4,2,8192]{2,1,0:T(2,128)S(1)} collective-permute-done((f32[4,2,8192]{2,1,0:T(2,128)S(1)}, f32[4,2,8192]{2,1,0:T(2,128)S(1)}, u32[]{:S(2)}, u32[]{:S(2)}) %collective-permute-start.4) | collective-permute-done | bytes 262176 | tf_op jit(solution)/shard_map/ppermute | solution.py:23
  90.0 1.5 collective-permute-done.5
  91.8 2.0 fusion.55
  94.2 1.1 fusion.56
  95.3 0.8 fusion.29
  96.1 1.0 copy.16
  97.1 3.1 %gather_fusion = f32[512]{0:T(512)S(1)} fusion(f32[65536]{0:T(1024)S(1)} %bitcast.247, s32[1024]{0:T(1024)S(1)} %pad_clamp_fusion), kind=kCustom, calls=%fused_computation | custom fusion | bytes 6144 | tf_op jit(solution)/shard_map/jit(_take)/gather | solution.py:131
  100.3 3.9 %scatter_custom_fusion.2 = f32[65536]{0:T(1024)} fusion(s32[512]{0:T(512)S(1)} %bitcast.260, f32[512]{0:T(512)S(1)} %subtract_select_fusion, f32[]{:T(128)} %constant.144.clone.1), kind=kCustom, calls=%fused_computation.127 | custom fusion | flops 512 | bytes 262148 | tf_op jit(solution)/shard_map/scatter-add | solution.py:136
  104.2 1.0 reshape.257
  105.3 1.3 fusion.53
  106.8 1.7 fusion
  108.6 0.7 add_add_fusion.1
  110.2 6.5 %collective-permute-start.6 = (f32[3,2,8192]{2,1,0:T(2,128)S(1)}, f32[3,2,8192]{2,1,0:T(2,128)S(1)}, u32[]{:S(2)}, u32[]{:S(2)}) collective-permute-start(f32[3,2,8192]{2,1,0:T(2,128)S(1)} %get-tuple-element.85), channel_id=1, source_target_pairs={{1,0},{2,1},{3,2},{4,3},{5,4},{6,5},{7,6},{8,7},{9,8},{10,9},{11,1... | collective-permute-start | bytes 589832 | tf_op jit(solution)/shard_map/ppermute | solution.py:12
  116.9 2.1 collective-permute-start.7
  119.0 0.9 collective-permute-done.6
  120.1 6.6 %collective-permute-done.7 = f32[3,2,8192]{2,1,0:T(2,128)S(1)} collective-permute-done((f32[3,2,8192]{2,1,0:T(2,128)S(1)}, f32[3,2,8192]{2,1,0:T(2,128)S(1)}, u32[]{:S(2)}, u32[]{:S(2)}) %collective-permute-start.7) | collective-permute-done | bytes 196640 | tf_op jit(solution)/shard_map/ppermute | solution.py:12
  127.1 1.5 fusion.1
  128.9 1.9 collective-permute-start.8
  130.8 3.9 %collective-permute-start.9 = (f32[1,2,8192]{2,1,0:T(2,128)S(1)}, f32[1,2,8192]{2,1,0:T(2,128)S(1)}, u32[]{:S(2)}, u32[]{:S(2)}) collective-permute-start(f32[1,2,8192]{2,1,0:T(2,128)S(1)} %get-tuple-element.92), channel_id=1, source_target_pairs={{0,1},{1,2},{2,3},{3,4},{4,5},{5,6},{6,7},{7,8},{8,9},{9,10},{10,1... | collective-permute-start | bytes 196616 | tf_op jit(solution)/shard_map/ppermute | solution.py:12
  135.1 4.0 %collective-permute-done.9 = f32[1,2,8192]{2,1,0:T(2,128)S(1)} collective-permute-done((f32[1,2,8192]{2,1,0:T(2,128)S(1)}, f32[1,2,8192]{2,1,0:T(2,128)S(1)}, u32[]{:S(2)}, u32[]{:S(2)}) %collective-permute-start.9) | collective-permute-done | bytes 65568 | tf_op jit(solution)/shard_map/ppermute | solution.py:12
  139.2 0.7 copy-done.22
  139.9 69.4 %all-reduce.30.cloned.1.call-done = f32[8,8192]{1,0:T(8,128)} async-done(((f32[8,8192]{1,0:T(8,128)}), f32[8,8192]{1,0:T(8,128)}) %all-reduce.30.cloned.1.call-update) | async-done | bytes 262160 | tf_op jit(solution)/shard_map/psum | solution.py:158
  209.3 1.4 constant_dynamic-slice_fusion
  (95 shorter events, 7.7 us)
Async XLA Ops:
  6.5 51.3 %copy-start.9 = (f32[1,8,8192]{2,1,0:T(8,128)S(1)}, f32[1,8,8192]{2,1,0:T(8,128)}, u32[]{:S(2)}) copy-start(f32[1,8,8192]{2,1,0:T(8,128)} %param.18) | copy-start | bytes 786436
  6.5 51.3 %copy-start.12 = (f32[1,8,8192]{2,1,0:T(8,128)S(1)}, f32[1,8,8192]{2,1,0:T(8,128)}, u32[]{:S(2)}) copy-start(f32[1,8,8192]{2,1,0:T(8,128)} %param.19) | copy-start | bytes 786436
  6.5 51.4 %copy-start.10 = (f32[1,8,8192]{2,1,0:T(8,128)S(1)}, f32[1,8,8192]{2,1,0:T(8,128)}, u32[]{:S(2)}) copy-start(f32[1,8,8192]{2,1,0:T(8,128)} %param.20) | copy-start | bytes 786436
  7.9 64.8 %collective-permute-start = (f32[2,2,8192]{2,1,0:T(2,128)S(1)}, f32[2,2,8192]{2,1,0:T(2,128)S(1)}, u32[]{:S(2)}, u32[]{:S(2)}) collective-permute-start(f32[2,2,8192]{2,1,0:T(2,128)S(1)} %get-tuple-element.102), channel_id=1, source_target_pairs={{0,1},{1,2},{2,3},{3,4},{4,5},{5,6},{6,7},{7,8},{8,9},{9,10},{10,1... | collective-permute-start | bytes 393224 | tf_op jit(solution)/shard_map/ppermute | solution.py:23
  11.7 61.0 %collective-permute-start.1 = (f32[2,2,8192]{2,1,0:T(2,128)S(1)}, f32[2,2,8192]{2,1,0:T(2,128)}, u32[]{:S(2)}, u32[]{:S(2)}) collective-permute-start(f32[2,2,8192]{2,1,0:T(2,128)S(1)} %get-tuple-element.103), channel_id=1, source_target_pairs={{1,0},{2,1},{3,2},{4,3},{5,4},{6,5},{7,6},{8,7},{9,8},{10,9},{11,1... | collective-permute-start | bytes 393224 | tf_op jit(solution)/shard_map/ppermute | solution.py:25
  26.5 25.9 %all-to-all-start = ((s32[64,1,8]{2,1,0:T(1,128)}), s32[64,1,8]{2,1,0:T(1,128)S(1)}, u32[]{:S(2)}, u32[]{:S(2)}) async-start(s32[64,1,8]{2,1,0:T(1,128)} %bitcast.12), calls=%async_computation | async-start | bytes 65536 | tf_op jit(solution)/shard_map/all_to_all | solution.py:114
  40.0 39.3 %copy-start.2 = (f32[1,2,8,8192]{3,2,1,0:T(8,128)}, f32[1,2,8,8192]{3,2,1,0:T(8,128)S(1)}, u32[]{:S(2)}) copy-start(f32[1,2,8,8192]{3,2,1,0:T(8,128)S(1)} %convert_element_type.19) | copy-start | bytes 1572868
  52.4 19.0 %all-to-all-start.1 = ((f32[64,1,8]{2,1,0:T(1,128)}), f32[64,1,8]{2,1,0:T(1,128)S(1)}, u32[]{:S(2)}, u32[]{:S(2)}) async-start(f32[64,1,8]{2,1,0:T(1,128)} %bitcast.32), calls=%async_computation.1 | async-start | bytes 65536 | tf_op jit(solution)/shard_map/all_to_all | solution.py:121
  57.8 151.5 %all-reduce.30.cloned.1.call-start = ((), (), s32[]{:S(2)}) async-start(), calls=%async_computation.2 | async-start | bytes 524288 | tf_op jit(solution)/shard_map/psum | solution.py:158
  58.9 15.1 %collective-permute-start.2 = (f32[4,2,8192]{2,1,0:T(2,128)}, f32[4,2,8192]{2,1,0:T(2,128)S(1)}, u32[]{:S(2)}, u32[]{:S(2)}) collective-permute-start(f32[4,2,8192]{2,1,0:T(2,128)} %get-tuple-element.88), channel_id=1, source_target_pairs={{0,1},{1,2},{2,3},{3,4},{4,5},{5,6},{6,7},{7,8},{8,9},{9,10},{10,1... | collective-permute-start | bytes 786440 | tf_op jit(solution)/shard_map/ppermute | solution.py:23
  62.2 11.8 %collective-permute-start.3 = (f32[4,2,8192]{2,1,0:T(2,128)}, f32[4,2,8192]{2,1,0:T(2,128)S(1)}, u32[]{:S(2)}, u32[]{:S(2)}) collective-permute-start(f32[4,2,8192]{2,1,0:T(2,128)} %get-tuple-element.89), channel_id=1, source_target_pairs={{1,0},{2,1},{3,2},{4,3},{5,4},{6,5},{7,6},{8,7},{9,8},{10,9},{11,1... | collective-permute-start | bytes 786440 | tf_op jit(solution)/shard_map/ppermute | solution.py:25
  74.0 0.7 copy-start.18
  74.7 0.7 copy-start.20
  75.7 2.1 copy-start
  75.8 2.1 copy-start.11
  75.8 2.1 copy-start.13
  75.8 2.1 copy-start.19
  75.8 2.1 copy-start.21
  77.8 1.5 copy-start.7
  79.6 10.4 %collective-permute-start.4 = (f32[4,2,8192]{2,1,0:T(2,128)S(1)}, f32[4,2,8192]{2,1,0:T(2,128)S(1)}, u32[]{:S(2)}, u32[]{:S(2)}) collective-permute-start(f32[4,2,8192]{2,1,0:T(2,128)S(1)} %get-tuple-element.86), channel_id=1, source_target_pairs={{0,1},{1,2},{2,3},{3,4},{4,5},{5,6},{6,7},{7,8},{8,9},{9,10},{10,1... | collective-permute-start | bytes 786440 | tf_op jit(solution)/shard_map/ppermute | solution.py:23
  82.2 9.2 %collective-permute-start.5 = (f32[4,2,8192]{2,1,0:T(2,128)S(1)}, f32[4,2,8192]{2,1,0:T(2,128)S(1)}, u32[]{:S(2)}, u32[]{:S(2)}) collective-permute-start(f32[4,2,8192]{2,1,0:T(2,128)S(1)} %get-tuple-element.87), channel_id=1, source_target_pairs={{1,0},{2,1},{3,2},{4,3},{5,4},{6,5},{7,6},{8,7},{9,8},{10,9},{11,1... | collective-permute-start | bytes 786440 | tf_op jit(solution)/shard_map/ppermute | solution.py:25
  93.9 1.4 copy-start.5
  94.2 1.1 copy-start.3
  105.2 1.4 copy-start.6
  105.2 1.4 copy-start.16
  105.3 1.6 copy-start.17
  110.2 9.7 %collective-permute-start.6 = (f32[3,2,8192]{2,1,0:T(2,128)S(1)}, f32[3,2,8192]{2,1,0:T(2,128)S(1)}, u32[]{:S(2)}, u32[]{:S(2)}) collective-permute-start(f32[3,2,8192]{2,1,0:T(2,128)S(1)} %get-tuple-element.85), channel_id=1, source_target_pairs={{1,0},{2,1},{3,2},{4,3},{5,4},{6,5},{7,6},{8,7},{9,8},{10,9},{11,1... | collective-permute-start | bytes 589832 | tf_op jit(solution)/shard_map/ppermute | solution.py:12
  116.8 10.1 %copy-start.4 = (f32[1,2,8,8192]{3,2,1,0:T(8,128)S(1)}, f32[1,2,8,8192]{3,2,1,0:T(8,128)}, u32[]{:S(2)}) copy-start(f32[1,2,8,8192]{3,2,1,0:T(8,128)} %copy-done.2) | copy-start | bytes 1572868
  116.9 9.8 %collective-permute-start.7 = (f32[3,2,8192]{2,1,0:T(2,128)S(1)}, f32[3,2,8192]{2,1,0:T(2,128)S(1)}, u32[]{:S(2)}, u32[]{:S(2)}) collective-permute-start(f32[3,2,8192]{2,1,0:T(2,128)S(1)} %get-tuple-element.84), channel_id=1, source_target_pairs={{0,1},{1,2},{2,3},{3,4},{4,5},{5,6},{6,7},{7,8},{8,9},{9,10},{10,1... | collective-permute-start | bytes 589832 | tf_op jit(solution)/shard_map/ppermute | solution.py:12
  120.1 7.0 %copy-start.1 = (f32[4,12,8192]{2,1,0:T(8,128)S(1)}, f32[4,12,8192]{2,1,0:T(8,128)}, u32[]{:S(2)}) copy-start(f32[4,12,8192]{2,1,0:T(8,128)} %copy-done) | copy-start | bytes 4718596
  120.1 7.0 %copy-start.8 = (f32[10,8192]{1,0:T(8,128)S(1)}, f32[10,8192]{1,0:T(8,128)}, u32[]{:S(2)}) copy-start(f32[10,8192]{1,0:T(8,128)} %copy-done.7) | copy-start | bytes 983044
  120.1 7.0 %copy-start.14 = (f32[10,8192]{1,0:T(8,128)S(1)}, f32[10,8192]{1,0:T(8,128)}, u32[]{:S(2)}) copy-start(f32[10,8192]{1,0:T(8,128)} %get-tuple-element.75) | copy-start | bytes 983044
  120.1 7.0 %copy-start.15 = (f32[10,8192]{1,0:T(8,128)S(1)}, f32[10,8192]{1,0:T(8,128)}, u32[]{:S(2)}) copy-start(f32[10,8192]{1,0:T(8,128)} %get-tuple-element.109) | copy-start | bytes 983044
  128.9 6.2 %collective-permute-start.8 = (f32[1,2,8192]{2,1,0:T(2,128)S(1)}, f32[1,2,8192]{2,1,0:T(2,128)S(1)}, u32[]{:S(2)}, u32[]{:S(2)}) collective-permute-start(f32[1,2,8192]{2,1,0:T(2,128)S(1)} %get-tuple-element.93), channel_id=1, source_target_pairs={{1,0},{2,1},{3,2},{4,3},{5,4},{6,5},{7,6},{8,7},{9,8},{10,9},{11,1... | collective-permute-start | bytes 196616 | tf_op jit(solution)/shard_map/ppermute | solution.py:12
  130.8 8.3 %collective-permute-start.9 = (f32[1,2,8192]{2,1,0:T(2,128)S(1)}, f32[1,2,8192]{2,1,0:T(2,128)S(1)}, u32[]{:S(2)}, u32[]{:S(2)}) collective-permute-start(f32[1,2,8192]{2,1,0:T(2,128)S(1)} %get-tuple-element.92), channel_id=1, source_target_pairs={{0,1},{1,2},{2,3},{3,4},{4,5},{5,6},{6,7},{7,8},{8,9},{9,10},{10,1... | collective-permute-start | bytes 196616 | tf_op jit(solution)/shard_map/ppermute | solution.py:12
  139.1 0.7 copy-start.22
Sparse Core Ops, SparseCore 0:
  140.0 69.2 all-reduce.29
where the time goes:
time: 218 us
  waiting for transfers between devices  98 us (45%)
  starting transfers between devices  61.7 us (28%)
  other arithmetic  28.1 us (13%)
  local copies, waits for them, and re-layouts  15.7 us (7%)
  between operations  14.1 us (6%)
    psum x1, waiting for transfers between devices, per_device(): total = lax.psum(local_grad, 'event')  69.4 us
    ppermute x3, starting transfers between devices, padded_2(): lax.ppermute(head, axis, [((i + 1) % count, i) for i in range(ends)])  19.6 us
    ppermute x4, starting transfers between devices, shifted(): lax.ppermute(value, axis, [(source, source + steps) for source in range(i...  14.4 us
    all_to_all x1, starting transfers between devices, per_device(): lax.all_to_all(send_cells.reshape(tile_count, capacity), 'tile', split_ax...  12.4 us
    ppermute x4, waiting for transfers between devices, shifted(): lax.ppermute(value, axis, [(source, source + steps) for source in range(i...  11.8 us
    all_to_all x1, waiting for transfers between devices, per_device(): lax.all_to_all(send_cells.reshape(tile_count, capacity), 'tile', split_ax...  10.1 us
    ppermute x3, starting transfers between devices, padded_2(): lax.ppermute(tail, axis, [(i, (i + 1) % count) for i in range(ends)])  9.78 us
    all_to_all x1, starting transfers between devices, per_device(): lax.all_to_all(send_values.reshape(tile_count, capacity), 'tile', split_a...  5.45 us
  transfers between devices with their start and end apart: 13, of which 9 were waited for; matrix products, arithmetic and copies ran while one was open for 6% of the time, Pallas kernels for 0%

commit v1 on v0

--- a/solution.py
+++ b/solution.py
@@ -81,6 +81,10 @@
     gauge_values,
     survey_surface,
 ):
+
+    def find_patch_on_mesh(xx):
+        return lax.all_gather(xx, axis_name="event").sum(axis=0)
+
     row_count, col_count = still_depth.shape
     wet_float = wet_masks[0].astype(jnp.float32)
     statics = jnp.stack((still_depth, roughness))
@@ -155,7 +159,7 @@
             folded = fold_rims(jnp.stack((back_surface, back_east, back_north)), 2)
             sense_surface, sense_east, sense_north = (folded[0], folded[1], folded[2])
     local_grad = fold_rims(rough_sense[None], width)[0]
-    total = lax.psum(local_grad, "event")
+    total = find_patch_on_mesh(local_grad)
     share = col_count // lax.axis_size("event")
     return lax.dynamic_slice_in_dim(total, lax.axis_index("event") * share, share, 1)
 

time: 218 us -> 178 us (0.82)
  the two profiles are of different devices: /device:TPU:2 before, /device:TPU:1 now
where the time goes in v1:
time: 178 us; the launch traced here: 177 us
  waiting for transfers between devices  68.8 us (39%)
  starting transfers between devices  49.2 us (28%)
  other arithmetic  29.8 us (17%)
  local copies, waits for them, and re-layouts  14.9 us (8%)
  between operations  14.1 us (8%)
    all_gather x1, waiting for transfers between devices, find_patch_on_mesh(): return lax.all_gather(xx, axis_name='event').sum(axis=0)  43.2 us
    all_to_all x1, starting transfers between devices, per_device(): lax.all_to_all(send_cells.reshape(tile_count, capacity), 'tile', split_ax...  19.9 us
    ppermute x4, starting transfers between devices, shifted(): lax.ppermute(value, axis, [(source, source + steps) for source in range(i...  11.2 us
    all_to_all x1, waiting for transfers between devices, per_device(): lax.all_to_all(send_cells.reshape(tile_count, capacity), 'tile', split_ax...  9.9 us
    ppermute x3, starting transfers between devices, padded_2(): lax.ppermute(tail, axis, [(i, (i + 1) % count) for i in range(ends)])  9.39 us
    all_to_all x1, waiting for transfers between devices, per_device(): lax.all_to_all(send_values.reshape(tile_count, capacity), 'tile', split_a...  6.53 us
    all_to_all x1, starting transfers between devices, per_device(): lax.all_to_all(send_values.reshape(tile_count, capacity), 'tile', split_a...  4.67 us
    ppermute x3, starting transfers between devices, padded_2(): lax.ppermute(head, axis, [((i + 1) % count, i) for i in range(ends)])  4.06 us
  transfers between devices with their start and end apart: 13, of which 8 were waited for; matrix products, arithmetic and copies ran while one was open for 7% of the time, Pallas kernels for 0%

profile of v1, /device:TPU:1, one launch (start us, length us, event | category | flops | bytes accessed | tf_op | source)
XLA Modules:
  0.0 176.9 jit_solution(5764286779834283115)
XLA Ops:
  6.5 1.4 pad_maximum_fusion.31
  7.9 4.4 %collective-permute-start = (f32[2,2,8192]{2,1,0:T(2,128)S(1)}, f32[2,2,8192]{2,1,0:T(2,128)S(1)}, u32[]{:S(2)}, u32[]{:S(2)}) collective-permute-start(f32[2,2,8192]{2,1,0:T(2,128)S(1)} %get-tuple-element.102), channel_id=1, source_target_pairs={{0,1},{1,2},{2,3},{3,4},{4,5},{5,6},{6,7},{7,8},{8,9},{9,10},{10,1... | collective-permute-start | bytes 393224 | tf_op jit(solution)/shard_map/ppermute | solution.py:23
  12.3 1.3 collective-permute-start.1
  13.6 0.7 fusion.43
  15.1 0.8 fusion.40
  16.6 1.6 scatter_custom_fusion
  18.1 0.7 all_to_all.12
  18.8 19.9 %all-to-all-start = ((s32[64,1,8]{2,1,0:T(1,128)}), s32[64,1,8]{2,1,0:T(1,128)S(1)}, u32[]{:S(2)}, u32[]{:S(2)}) async-start(s32[64,1,8]{2,1,0:T(1,128)} %bitcast.12), calls=%async_computation | async-start | bytes 65536 | tf_op jit(solution)/shard_map/all_to_all | solution.py:118
  38.8 1.1 convert_element_type.19
  39.9 1.6 scatter_custom_fusion.1
  41.5 0.7 all_to_all.14
  42.2 9.9 %all-to-all-done = s32[64,1,8]{2,1,0:T(1,128)S(1)} async-done(((s32[64,1,8]{2,1,0:T(1,128)}), s32[64,1,8]{2,1,0:T(1,128)S(1)}, u32[]{:S(2)}, u32[]{:S(2)}) %all-to-all-start) | async-done | bytes 2080 | tf_op jit(solution)/shard_map/all_to_all | solution.py:118
  52.1 4.7 %all-to-all-start.1 = ((f32[64,1,8]{2,1,0:T(1,128)}), f32[64,1,8]{2,1,0:T(1,128)S(1)}, u32[]{:S(2)}, u32[]{:S(2)}) async-start(f32[64,1,8]{2,1,0:T(1,128)} %bitcast.32), calls=%async_computation.1 | async-start | bytes 65536 | tf_op jit(solution)/shard_map/all_to_all | solution.py:125
  56.8 1.0 pad_maximum_fusion.27
  57.8 2.9 %collective-permute-start.2 = (f32[4,2,8192]{2,1,0:T(2,128)}, f32[4,2,8192]{2,1,0:T(2,128)S(1)}, u32[]{:S(2)}, u32[]{:S(2)}) collective-permute-start(f32[4,2,8192]{2,1,0:T(2,128)} %get-tuple-element.88), channel_id=1, source_target_pairs={{0,1},{1,2},{2,3},{3,4},{4,5},{5,6},{6,7},{7,8},{8,9},{9,10},{10,1... | collective-permute-start | bytes 786440 | tf_op jit(solution)/shard_map/ppermute | solution.py:23
  60.7 1.3 collective-permute-start.3
  62.6 0.7 reduce.18
  63.5 6.5 %all-to-all-done.1 = f32[64,1,8]{2,1,0:T(1,128)S(1)} async-done(((f32[64,1,8]{2,1,0:T(1,128)}), f32[64,1,8]{2,1,0:T(1,128)S(1)}, u32[]{:S(2)}, u32[]{:S(2)}) %all-to-all-start.1) | async-done | bytes 2080 | tf_op jit(solution)/shard_map/all_to_all | solution.py:125
  70.6 0.7 reduce.19
  71.4 1.3 pad_maximum_fusion.3
  73.4 0.7 copy-done.21
  74.5 2.0 %fusion.57 = (f32[10,8192]{1,0:T(8,128)S(1)}, f32[10,8192]{1,0:T(8,128)S(1)}, f32[10,8192]{1,0:T(8,128)}) fusion(f32[2,12,8192]{2,1,0:T(8,128)S(1)} %pad_maximum_fusion.3, f32[4,12,8192]{2,1,0:T(8,128)S(1)} %pad_maximum_fusion, f32[10,8192]{1,0:T(8,128)S(1)} %slice_bitcast_fusion.5), kind=kLoop, calls=%fused_computation.161 | loop fusion | flops 1392640 | bytes 2949120 | tf_op jit(solution)/shard_map/div | solution.py:54
  76.6 1.4 pad_slice_fusion.3
  78.3 2.1 %collective-permute-start.4 = (f32[4,2,8192]{2,1,0:T(2,128)S(1)}, f32[4,2,8192]{2,1,0:T(2,128)S(1)}, u32[]{:S(2)}, u32[]{:S(2)}) collective-permute-start(f32[4,2,8192]{2,1,0:T(2,128)S(1)} %get-tuple-element.86), channel_id=1, source_target_pairs={{0,1},{1,2},{2,3},{3,4},{4,5},{5,6},{6,7},{7,8},{8,9},{9,10},{10,1... | collective-permute-start | bytes 786440 | tf_op jit(solution)/shard_map/ppermute | solution.py:23
  80.4 1.5 collective-permute-start.5
  81.9 1.8 %collective-permute-done.4 = f32[4,2,8192]{2,1,0:T(2,128)S(1)} collective-permute-done((f32[4,2,8192]{2,1,0:T(2,128)S(1)}, f32[4,2,8192]{2,1,0:T(2,128)S(1)}, u32[]{:S(2)}, u32[]{:S(2)}) %collective-permute-start.4) | collective-permute-done | bytes 262176 | tf_op jit(solution)/shard_map/ppermute | solution.py:23
  83.7 3.8 %collective-permute-done.5 = f32[4,2,8192]{2,1,0:T(2,128)S(1)} collective-permute-done((f32[4,2,8192]{2,1,0:T(2,128)S(1)}, f32[4,2,8192]{2,1,0:T(2,128)S(1)}, u32[]{:S(2)}, u32[]{:S(2)}) %collective-permute-start.5) | collective-permute-done | bytes 262176 | tf_op jit(solution)/shard_map/ppermute | solution.py:25
  87.9 2.0 %fusion.54 = (f32[10,8192]{1,0:T(8,128)S(1)}, f32[10,8192]{1,0:T(8,128)}, f32[10,8192]{1,0:T(8,128)S(1)}) fusion(f32[10,8192]{1,0:T(8,128)S(1)} %slice_bitcast_fusion.1, f32[2,12,8192]{2,1,0:T(8,128)S(1)} %pad_maximum_fusion.3, f32[4,12,8192]{2,1,0:T(8,128)S(1)} %pad_maximum_fusion.1), kind=kLoop, calls=%fused_computation.159 | loop fusion | flops 1392640 | bytes 2949120 | tf_op jit(solution)/shard_map/div | solution.py:54
  90.3 1.1 fusion.55
  91.4 0.8 fusion.29
  92.2 1.0 copy.16
  93.2 3.1 %gather_fusion = f32[512]{0:T(512)S(1)} fusion(f32[65536]{0:T(1024)S(1)} %bitcast.242, s32[1024]{0:T(1024)S(1)} %pad_clamp_fusion), kind=kCustom, calls=%fused_computation | custom fusion | bytes 6144 | tf_op jit(solution)/shard_map/jit(_take)/gather | solution.py:135
  96.4 3.9 %scatter_custom_fusion.2 = f32[65536]{0:T(1024)} fusion(s32[512]{0:T(512)S(1)} %bitcast.254, f32[512]{0:T(512)S(1)} %subtract_select_fusion, f32[]{:T(128)} %constant.143.clone.1), kind=kCustom, calls=%fused_computation.127 | custom fusion | flops 512 | bytes 262148 | tf_op jit(solution)/shard_map/scatter-add | solution.py:140
  100.3 1.0 reshape.255
  101.4 1.3 fusion.52
  102.9 1.7 fusion
  104.7 0.7 add_add_fusion.1
  106.3 1.3 collective-permute-start.6
  107.8 4.1 %collective-permute-start.7 = (f32[3,2,8192]{2,1,0:T(2,128)S(1)}, f32[3,2,8192]{2,1,0:T(2,128)S(1)}, u32[]{:S(2)}, u32[]{:S(2)}) collective-permute-start(f32[3,2,8192]{2,1,0:T(2,128)S(1)} %get-tuple-element.84), channel_id=1, source_target_pairs={{0,1},{1,2},{2,3},{3,4},{4,5},{5,6},{6,7},{7,8},{8,9},{9,10},{10,1... | collective-permute-start | bytes 589832 | tf_op jit(solution)/shard_map/ppermute | solution.py:12
  111.9 0.8 collective-permute-done.6
  112.9 1.6 collective-permute-done.7
  114.9 1.5 fusion.1
  116.7 1.3 collective-permute-start.8
  118.0 4.4 %collective-permute-start.9 = (f32[1,2,8192]{2,1,0:T(2,128)S(1)}, f32[1,2,8192]{2,1,0:T(2,128)S(1)}, u32[]{:S(2)}, u32[]{:S(2)}) collective-permute-start(f32[1,2,8192]{2,1,0:T(2,128)S(1)} %get-tuple-element.92), channel_id=1, source_target_pairs={{0,1},{1,2},{2,3},{3,4},{4,5},{5,6},{6,7},{7,8},{8,9},{9,10},{10,1... | collective-permute-start | bytes 196616 | tf_op jit(solution)/shard_map/ppermute | solution.py:12
  122.5 1.2 collective-permute-done.9
  123.8 0.7 copy-done.18
  124.5 43.2 %all-gather.2.cloned.1.call-done = f32[8,8,8192]{2,1,0:T(8,128)} async-done(((f32[1,8,8192]{2,1,0:T(8,128)}), f32[8,8,8192]{2,1,0:T(8,128)}) %all-gather.2.cloned.1.call-update) | async-done | bytes 2097168 | tf_op jit(solution)/shard_map/all_gather | solution.py:86
  167.7 1.7 reduce_sum.22
  (95 shorter events, 8.0 us)
Async XLA Ops:
  6.5 50.3 %copy-start.9 = (f32[1,8,8192]{2,1,0:T(8,128)S(1)}, f32[1,8,8192]{2,1,0:T(8,128)}, u32[]{:S(2)}) copy-start(f32[1,8,8192]{2,1,0:T(8,128)} %param.18) | copy-start | bytes 786436
  6.5 50.3 %copy-start.12 = (f32[1,8,8192]{2,1,0:T(8,128)S(1)}, f32[1,8,8192]{2,1,0:T(8,128)}, u32[]{:S(2)}) copy-start(f32[1,8,8192]{2,1,0:T(8,128)} %param.19) | copy-start | bytes 786436
  6.5 50.3 %copy-start.10 = (f32[1,8,8192]{2,1,0:T(8,128)S(1)}, f32[1,8,8192]{2,1,0:T(8,128)}, u32[]{:S(2)}) copy-start(f32[1,8,8192]{2,1,0:T(8,128)} %param.20) | copy-start | bytes 786436
  7.9 63.5 %collective-permute-start = (f32[2,2,8192]{2,1,0:T(2,128)S(1)}, f32[2,2,8192]{2,1,0:T(2,128)S(1)}, u32[]{:S(2)}, u32[]{:S(2)}) collective-permute-start(f32[2,2,8192]{2,1,0:T(2,128)S(1)} %get-tuple-element.102), channel_id=1, source_target_pairs={{0,1},{1,2},{2,3},{3,4},{4,5},{5,6},{6,7},{7,8},{8,9},{9,10},{10,1... | collective-permute-start | bytes 393224 | tf_op jit(solution)/shard_map/ppermute | solution.py:23
  12.3 59.1 %collective-permute-start.1 = (f32[2,2,8192]{2,1,0:T(2,128)S(1)}, f32[2,2,8192]{2,1,0:T(2,128)}, u32[]{:S(2)}, u32[]{:S(2)}) collective-permute-start(f32[2,2,8192]{2,1,0:T(2,128)S(1)} %get-tuple-element.103), channel_id=1, source_target_pairs={{1,0},{2,1},{3,2},{4,3},{5,4},{6,5},{7,6},{8,7},{9,8},{10,9},{11,1... | collective-permute-start | bytes 393224 | tf_op jit(solution)/shard_map/ppermute | solution.py:25
  18.8 33.2 %all-to-all-start = ((s32[64,1,8]{2,1,0:T(1,128)}), s32[64,1,8]{2,1,0:T(1,128)S(1)}, u32[]{:S(2)}, u32[]{:S(2)}) async-start(s32[64,1,8]{2,1,0:T(1,128)} %bitcast.12), calls=%async_computation | async-start | bytes 65536 | tf_op jit(solution)/shard_map/all_to_all | solution.py:118
  39.9 38.1 %copy-start.2 = (f32[1,2,8,8192]{3,2,1,0:T(8,128)}, f32[1,2,8,8192]{3,2,1,0:T(8,128)S(1)}, u32[]{:S(2)}) copy-start(f32[1,2,8,8192]{3,2,1,0:T(8,128)S(1)} %convert_element_type.19) | copy-start | bytes 1572868
  52.1 18.0 %all-to-all-start.1 = ((f32[64,1,8]{2,1,0:T(1,128)}), f32[64,1,8]{2,1,0:T(1,128)S(1)}, u32[]{:S(2)}, u32[]{:S(2)}) async-start(f32[64,1,8]{2,1,0:T(1,128)} %bitcast.32), calls=%async_computation.1 | async-start | bytes 65536 | tf_op jit(solution)/shard_map/all_to_all | solution.py:125
  56.7 111.0 %all-gather.2.cloned.1.call-start = ((), (), s32[]{:S(2)}) async-start(), calls=%async_computation.2 | async-start | bytes 2359296 | tf_op jit(solution)/shard_map/all_gather | solution.py:86
  57.8 14.9 %collective-permute-start.2 = (f32[4,2,8192]{2,1,0:T(2,128)}, f32[4,2,8192]{2,1,0:T(2,128)S(1)}, u32[]{:S(2)}, u32[]{:S(2)}) collective-permute-start(f32[4,2,8192]{2,1,0:T(2,128)} %get-tuple-element.88), channel_id=1, source_target_pairs={{0,1},{1,2},{2,3},{3,4},{4,5},{5,6},{6,7},{7,8},{8,9},{9,10},{10,1... | collective-permute-start | bytes 786440 | tf_op jit(solution)/shard_map/ppermute | solution.py:23
  60.7 12.0 %collective-permute-start.3 = (f32[4,2,8192]{2,1,0:T(2,128)}, f32[4,2,8192]{2,1,0:T(2,128)S(1)}, u32[]{:S(2)}, u32[]{:S(2)}) collective-permute-start(f32[4,2,8192]{2,1,0:T(2,128)} %get-tuple-element.89), channel_id=1, source_target_pairs={{1,0},{2,1},{3,2},{4,3},{5,4},{6,5},{7,6},{8,7},{9,8},{10,9},{11,1... | collective-permute-start | bytes 786440 | tf_op jit(solution)/shard_map/ppermute | solution.py:25
  72.7 0.7 copy-start.19
  73.4 0.7 copy-start.21
  74.4 2.1 %copy-start = (f32[4,12,8192]{2,1,0:T(8,128)}, f32[4,12,8192]{2,1,0:T(8,128)S(1)}, u32[]{:S(2)}) copy-start(f32[4,12,8192]{2,1,0:T(8,128)S(1)} %pad_maximum_fusion) | copy-start | bytes 4718596
  74.5 2.1 %copy-start.11 = (f32[1,8,8192]{2,1,0:T(8,128)S(1)}, f32[1,8,8192]{2,1,0:T(8,128)}, u32[]{:S(2)}) copy-start(f32[1,8,8192]{2,1,0:T(8,128)} %param.20) | copy-start | bytes 786436
  74.5 2.1 %copy-start.13 = (f32[1,8,8192]{2,1,0:T(8,128)S(1)}, f32[1,8,8192]{2,1,0:T(8,128)}, u32[]{:S(2)}) copy-start(f32[1,8,8192]{2,1,0:T(8,128)} %param.19) | copy-start | bytes 786436
  74.5 2.1 %copy-start.20 = (f32[4,2,8192]{2,1,0:T(2,128)S(1)}, f32[4,2,8192]{2,1,0:T(2,128)}, u32[]{:S(2)}) copy-start(f32[4,2,8192]{2,1,0:T(2,128)} %copy-done.19) | copy-start | bytes 786436
  74.5 2.1 %copy-start.22 = (f32[4,2,8192]{2,1,0:T(2,128)S(1)}, f32[4,2,8192]{2,1,0:T(2,128)}, u32[]{:S(2)}) copy-start(f32[4,2,8192]{2,1,0:T(2,128)} %copy-done.21) | copy-start | bytes 786436
  76.5 1.5 copy-start.7
  78.3 5.4 %collective-permute-start.4 = (f32[4,2,8192]{2,1,0:T(2,128)S(1)}, f32[4,2,8192]{2,1,0:T(2,128)S(1)}, u32[]{:S(2)}, u32[]{:S(2)}) collective-permute-start(f32[4,2,8192]{2,1,0:T(2,128)S(1)} %get-tuple-element.86), channel_id=1, source_target_pairs={{0,1},{1,2},{2,3},{3,4},{4,5},{5,6},{6,7},{7,8},{8,9},{9,10},{10,1... | collective-permute-start | bytes 786440 | tf_op jit(solution)/shard_map/ppermute | solution.py:23
  80.4 7.1 %collective-permute-start.5 = (f32[4,2,8192]{2,1,0:T(2,128)S(1)}, f32[4,2,8192]{2,1,0:T(2,128)S(1)}, u32[]{:S(2)}, u32[]{:S(2)}) collective-permute-start(f32[4,2,8192]{2,1,0:T(2,128)S(1)} %get-tuple-element.87), channel_id=1, source_target_pairs={{1,0},{2,1},{3,2},{4,3},{5,4},{6,5},{7,6},{8,7},{9,8},{10,9},{11,1... | collective-permute-start | bytes 786440 | tf_op jit(solution)/shard_map/ppermute | solution.py:25
  89.9 1.4 copy-start.5
  90.3 1.1 copy-start.3
  101.3 1.4 copy-start.6
  101.3 1.4 copy-start.16
  101.3 1.6 copy-start.17
  106.3 6.4 %collective-permute-start.6 = (f32[3,2,8192]{2,1,0:T(2,128)S(1)}, f32[3,2,8192]{2,1,0:T(2,128)S(1)}, u32[]{:S(2)}, u32[]{:S(2)}) collective-permute-start(f32[3,2,8192]{2,1,0:T(2,128)S(1)} %get-tuple-element.85), channel_id=1, source_target_pairs={{1,0},{2,1},{3,2},{4,3},{5,4},{6,5},{7,6},{8,7},{9,8},{10,9},{11,1... | collective-permute-start | bytes 589832 | tf_op jit(solution)/shard_map/ppermute | solution.py:12
  107.7 7.0 %copy-start.4 = (f32[1,2,8,8192]{3,2,1,0:T(8,128)S(1)}, f32[1,2,8,8192]{3,2,1,0:T(8,128)}, u32[]{:S(2)}) copy-start(f32[1,2,8,8192]{3,2,1,0:T(8,128)} %copy-done.2) | copy-start | bytes 1572868
  107.8 6.7 %collective-permute-start.7 = (f32[3,2,8192]{2,1,0:T(2,128)S(1)}, f32[3,2,8192]{2,1,0:T(2,128)S(1)}, u32[]{:S(2)}, u32[]{:S(2)}) collective-permute-start(f32[3,2,8192]{2,1,0:T(2,128)S(1)} %get-tuple-element.84), channel_id=1, source_target_pairs={{0,1},{1,2},{2,3},{3,4},{4,5},{5,6},{6,7},{7,8},{8,9},{9,10},{10,1... | collective-permute-start | bytes 589832 | tf_op jit(solution)/shard_map/ppermute | solution.py:12
  112.9 2.0 %copy-start.1 = (f32[4,12,8192]{2,1,0:T(8,128)S(1)}, f32[4,12,8192]{2,1,0:T(8,128)}, u32[]{:S(2)}) copy-start(f32[4,12,8192]{2,1,0:T(8,128)} %copy-done) | copy-start | bytes 4718596
  112.9 2.0 %copy-start.8 = (f32[10,8192]{1,0:T(8,128)S(1)}, f32[10,8192]{1,0:T(8,128)}, u32[]{:S(2)}) copy-start(f32[10,8192]{1,0:T(8,128)} %copy-done.7) | copy-start | bytes 983044
  112.9 2.0 %copy-start.14 = (f32[10,8192]{1,0:T(8,128)S(1)}, f32[10,8192]{1,0:T(8,128)}, u32[]{:S(2)}) copy-start(f32[10,8192]{1,0:T(8,128)} %get-tuple-element.75) | copy-start | bytes 983044
  112.9 2.0 %copy-start.15 = (f32[10,8192]{1,0:T(8,128)S(1)}, f32[10,8192]{1,0:T(8,128)}, u32[]{:S(2)}) copy-start(f32[10,8192]{1,0:T(8,128)} %get-tuple-element.109) | copy-start | bytes 983044
  116.7 5.8 %collective-permute-start.8 = (f32[1,2,8192]{2,1,0:T(2,128)S(1)}, f32[1,2,8192]{2,1,0:T(2,128)S(1)}, u32[]{:S(2)}, u32[]{:S(2)}) collective-permute-start(f32[1,2,8192]{2,1,0:T(2,128)S(1)} %get-tuple-element.93), channel_id=1, source_target_pairs={{1,0},{2,1},{3,2},{4,3},{5,4},{6,5},{7,6},{8,7},{9,8},{10,9},{11,1... | collective-permute-start | bytes 196616 | tf_op jit(solution)/shard_map/ppermute | solution.py:12
  118.0 5.8 %collective-permute-start.9 = (f32[1,2,8192]{2,1,0:T(2,128)S(1)}, f32[1,2,8192]{2,1,0:T(2,128)S(1)}, u32[]{:S(2)}, u32[]{:S(2)}) collective-permute-start(f32[1,2,8192]{2,1,0:T(2,128)S(1)} %get-tuple-element.92), channel_id=1, source_target_pairs={{0,1},{1,2},{2,3},{3,4},{4,5},{5,6},{6,7},{7,8},{8,9},{9,10},{10,1... | collective-permute-start | bytes 196616 | tf_op jit(solution)/shard_map/ppermute | solution.py:12
  123.8 0.7 copy-start.18
Sparse Core Ops, SparseCore 0:
  124.7 43.0 all-gather.1
